TPU v7x, 32 devices: a whole 2x2x4 slice. The times are simulated.
32 devices in a mesh: gx: 4 (over z), gy: 4 (over x, core), gz: 2 (over y).
Axes of the slice: x: 2, y: 2, z: 4, core: 2. Of those that a mesh axis runs over, the one named last changes fastest.
Arguments:
- response: float32 [32, 32, 12, 128], P('gx', 'gy', 'gz'), may hold values from -3 to 3
- source: float32 [32, 32, 12, 128], P('gx', 'gy', 'gz'), may hold values from -6 to 6
- occupied: float32 [32, 32, 12, 2048], P('gx', 'gy', 'gz'), may hold values from -0.0546875 to 0.0546875
- potential: float32 [32, 32, 12], P('gx', 'gy', 'gz'), may hold values from 0 to 2
- energy_shift: float32 [128], replicated, may hold values from 0.5 to 2
Outputs:
- updated: float32 [32, 32, 12, 128], P('gx', 'gy', 'gz')
- projected: float32 [32, 32, 12, 128], P('gx', 'gy', 'gz')
All inputs are finite; a program needn't handle non-finite values.
Results may differ from a plain program's by a relative error of at most 0.00011.
Values sent between devices are 32-bit elements; how exact they have to be, the bound alone decides.
No kernel may reach another device: no remote copies, remote signals or barrier semaphores. Data moves between devices by JAX's collectives and lax.ppermute only.
A program may use at most 64 MiB of HBM per device.

v0:
```python
import jax
import jax.numpy as jnp
from jax import lax
from jax.sharding import PartitionSpec as P

stencil_weights = (
    -5369.0 / 1800.0,
    12.0 / 7.0,
    -15.0 / 56.0,
    10.0 / 189.0,
    -1.0 / 112.0,
    2.0 / 1925.0,
    -1.0 / 16632.0,
)
damping = 0.1
margin = 6


def with_halo(block, sides, width):
    for axis, dim in sides:
        count = lax.axis_size(axis)
        forward = [(i, i + 1) for i in range(count - 1)]
        backward = [(target, source) for source, target in forward]
        low = lax.ppermute(
            lax.slice_in_dim(block, block.shape[dim] - width, None, axis=dim), axis, forward
        )
        high = lax.ppermute(lax.slice_in_dim(block, 0, width, axis=dim), axis, backward)
        block = jnp.concatenate([low, block, high], axis=dim)
    return block


def laplacian(padded, span_first, span_second, span_third):
    centre = padded[
        margin : margin + span_first, margin : margin + span_second, margin : margin + span_third
    ]
    summed = 3.0 * stencil_weights[0] * centre
    for offset in range(1, margin + 1):
        beside = padded[
            margin + offset : margin + offset + span_first,
            margin : margin + span_second,
            margin : margin + span_third,
        ]
        beside = (
            beside
            + padded[
                margin - offset : margin - offset + span_first,
                margin : margin + span_second,
                margin : margin + span_third,
            ]
        )
        beside = (
            beside
            + padded[
                margin : margin + span_first,
                margin + offset : margin + offset + span_second,
                margin : margin + span_third,
            ]
        )
        beside = (
            beside
            + padded[
                margin : margin + span_first,
                margin - offset : margin - offset + span_second,
                margin : margin + span_third,
            ]
        )
        beside = (
            beside
            + padded[
                margin : margin + span_first,
                margin : margin + span_second,
                margin + offset : margin + offset + span_third,
            ]
        )
        beside = (
            beside
            + padded[
                margin : margin + span_first,
                margin : margin + span_second,
                margin - offset : margin - offset + span_third,
            ]
        )
        summed = summed + stencil_weights[offset] * beside
    return (centre, summed)


def residual_of(padded, potential, energy_shift, source):
    span_first, span_second, span_third = potential.shape
    centre, summed = laplacian(padded, span_first, span_second, span_third)
    return -0.5 * summed + (potential[:, :, :, None] + energy_shift) * centre + source


def shards(response, source, occupied, potential, energy_shift):
    span_first, span_second, span_third, orbitals = response.shape
    cell_count = span_first * span_second * span_third
    flat_occ = occupied.reshape(cell_count, occupied.shape[3])
    updated = response
    padded = with_halo(updated, (("gx", 0), ("gy", 1), ("gz", 2)), 6)
    residual = residual_of(padded, potential, energy_shift, source)
    flat_res = residual.reshape(cell_count, orbitals)
    partial_intersection = lax.dot_general(
        flat_occ,
        flat_res,
        (((0,), (0,)), ((), ())),
        precision=lax.Precision.HIGHEST,
        preferred_element_type=jnp.float32,
    )
    share = lax.psum_scatter(partial_intersection, ("gy", "gz"), scatter_dimension=0, tiled=True)
    share = lax.psum(share, "gx")
    removed = jnp.dot(
        flat_occ,
        lax.all_gather(share, ("gy", "gz"), axis=0, tiled=True),
        precision=lax.Precision.HIGHEST,
        preferred_element_type=jnp.float32,
    )
    projected = (flat_res - removed).reshape(updated.shape)
    updated = updated - damping * projected
    return (updated, projected)


def solution(mesh):
    return jax.shard_map(
        shards,
        mesh=mesh,
        in_specs=(
            P("gx", "gy", "gz", None),
            P("gx", "gy", "gz", None),
            P("gx", "gy", "gz", None),
            P("gx", "gy", "gz"),
            P(),
        ),
        out_specs=(P("gx", "gy", "gz", None), P("gx", "gy", "gz", None)),
        check_vma=False,
    )
```

profile of v0, /device:TPU:0, one launch (start us, length us, event | category | flops | bytes accessed | tf_op | source)
XLA Modules:
  0.0 182.8 jit_solution(17553583483827970159)
XLA Ops:
  7.2 0.0 reduce-scatter.2.cloned.1.call-start
  7.2 1.0 fusion.49
  8.2 5.0 %collective-permute-start.1 = (f32[6,8,6,128]{3,1,2,0:T(8,128)S(1)}, f32[6,8,6,128]{3,1,2,0:T(8,128)S(1)}, u32[]{:S(2)}, u32[]{:S(2)}) collective-permute-start(f32[6,8,6,128]{3,1,2,0:T(8,128)S(1)} %get-tuple-element.12), channel_id=1, source_target_pairs={{0,8},{8,16},{16,24},{1,9},{9,17},{17,25},{2,10},{10,18},{18,26},{... | collective-permute-start | bytes 442376 | tf_op jit(solution)/shard_map/ppermute | solution.py:24
  13.2 1.3 collective-permute-start
  14.5 1.8 collective-permute-done.1
  16.3 1.0 constant_dynamic-update-slice_fusion.1
  17.3 3.1 %collective-permute-done = f32[6,8,6,128]{3,1,2,0:T(8,128)S(1)} collective-permute-done((f32[6,8,6,128]{3,1,2,0:T(8,128)S(1)}, f32[6,8,6,128]{3,1,2,0:T(8,128)S(1)}, u32[]{:S(2)}, u32[]{:S(2)}) %collective-permute-start) | collective-permute-done | bytes 147488 | tf_op jit(solution)/shard_map/ppermute | solution.py:27
  20.4 0.1 fusion.48
  20.5 1.3 collective-permute-start.2
  21.8 0.0 copy-start.3
  21.8 0.0 copy-start.1
  21.8 0.0 copy-start.2
  21.8 0.0 copy-start.4
  21.8 3.2 %collective-permute-start.3 = (f32[20,6,6,128]{3,1,2,0:T(8,128)S(1)}, f32[20,6,6,128]{3,1,2,0:T(8,128)S(1)}, u32[]{:S(2)}, u32[]{:S(2)}) collective-permute-start(f32[20,6,6,128]{3,1,2,0:T(8,128)S(1)} %get-tuple-element.7), channel_id=1, source_target_pairs={{0,2},{2,4},{4,6},{1,3},{3,5},{5,7},{8,10},{10,12},{12,14},{9,11},... | collective-permute-start | bytes 1105928 | tf_op jit(solution)/shard_map/ppermute | solution.py:24
  25.0 0.0 collective-permute-done.2
  25.1 1.4 collective-permute-done.3
  26.5 0.2 pad_maximum_fusion
  26.7 3.5 %collective-permute-start.5 = (f32[20,20,6,128]{3,1,2,0:T(8,128)S(1)}, f32[20,20,6,128]{3,1,2,0:T(8,128)S(1)}, u32[]{:S(2)}, u32[]{:S(2)}) collective-permute-start(f32[20,20,6,128]{3,1,2,0:T(8,128)S(1)} %pad_maximum_fusion), channel_id=1, source_target_pairs={{0,1},{2,3},{4,5},{6,7},{8,9},{10,11},{12,13},{14,15},{16,17},{18,... | collective-permute-start | bytes 3686408 | tf_op jit(solution)/shard_map/ppermute | solution.py:24
  30.2 1.3 collective-permute-start.4
  31.5 0.0 copy-done.3
  31.6 26.8 %collective-permute-done.5 = f32[20,20,6,128]{3,1,2,0:T(8,128)S(1)} collective-permute-done((f32[20,20,6,128]{3,1,2,0:T(8,128)S(1)}, f32[20,20,6,128]{3,1,2,0:T(8,128)S(1)}, u32[]{:S(2)}, u32[]{:S(2)}) %collective-permute-start.5) | collective-permute-done | bytes 1228832 | tf_op jit(solution)/shard_map/ppermute | solution.py:24
  58.4 4.8 %collective-permute-done.4 = f32[20,20,6,128]{3,1,2,0:T(8,128)S(1)} collective-permute-done((f32[20,20,6,128]{3,1,2,0:T(8,128)S(1)}, f32[20,20,6,128]{3,1,2,0:T(8,128)S(1)}, u32[]{:S(2)}, u32[]{:S(2)}) %collective-permute-start.4) | collective-permute-done | bytes 1228832 | tf_op jit(solution)/shard_map/ppermute | solution.py:27
  63.1 0.0 copy-done.1
  63.1 0.0 copy-done.2
  63.1 0.0 copy-done.4
  63.1 0.0 copy-start
  63.2 0.9 fusion.10
  64.1 1.0 copy-done
  65.0 3.0 %convolution_bitcast_fusion = f32[2048,128]{0,1:T(8,128)} fusion(f32[8,8,6,128]{3,1,2,0:T(8,128)S(1)} %fusion.10, f32[8,8,6,2048]{3,1,2,0:T(8,128)S(1)} %copy-done), kind=kOutput, calls=%fused_computation | convolution fusion | flops 1207959552 | bytes 4390912 | tf_op jit(solution)/shard_map/dot_general | solution.py:101
  68.1 0.0 reduce-scatter.2.cloned.1.call-update
  68.1 0.0 all-reduce.2.cloned.1.call-start
  68.1 38.7 %reduce-scatter.2.cloned.1.call-done = f32[256,128]{0,1:T(8,128)} async-done(((f32[2048,128]{0,1:T(8,128)}), f32[256,128]{0,1:T(8,128)}) %reduce-scatter.2.cloned.1.call-update) | async-done | bytes 131088 | tf_op jit(solution)/shard_map/reduce_scatter | solution.py:108
  106.8 0.0 all-reduce.2.cloned.1.call-update
  106.8 0.0 all-gather.2.cloned.1.call-start
  106.8 36.9 %all-reduce.2.cloned.1.call-done = f32[256,128]{0,1:T(8,128)} async-done(((f32[256,128]{0,1:T(8,128)}), f32[256,128]{0,1:T(8,128)}) %all-reduce.2.cloned.1.call-update) | async-done | bytes 131088 | tf_op jit(solution)/shard_map/psum | solution.py:109
  143.8 0.0 all-gather.2.cloned.1.call-update
  143.8 3.8 %copy.13 = f32[8,8,6,2048]{3,2,1,0:T(8,128)} copy(f32[8,8,6,2048]{3,1,2,0:T(8,128)S(1)} %copy-done) | data formatting | bytes 6291456 | tf_op args[2]
  147.6 3.1 %reshape.16 = f32[384,2048]{1,0:T(8,128)S(1)} reshape(f32[8,8,6,2048]{3,2,1,0:T(8,128)} %copy.13) | data formatting | bytes 6291456 | tf_op jit(solution)/shard_map/reshape | solution.py:96
  150.7 0.7 copy.12
  151.4 1.7 reshape.15
  153.1 1.1 copy.14
  154.1 14.8 %all-gather.2.cloned.1.call-done = f32[2048,128]{0,1:T(8,128)} async-done(((f32[256,128]{0,1:T(8,128)}), f32[2048,128]{0,1:T(8,128)}) %all-gather.2.cloned.1.call-update) | async-done | bytes 1048592 | tf_op jit(solution)/shard_map/all_gather | solution.py:112
  168.9 4.8 %fusion = f32[384,128]{0,1:T(8,128)} fusion(f32[384,128]{0,1:T(8,128)S(1)} %copy.14, f32[2048,128]{0,1:T(8,128)} %all-gather.2.cloned.1.call-done, f32[384,2048]{1,0:T(8,128)S(1)} %reshape.16), kind=kOutput, calls=%fused_computation.23 | convolution fusion | flops 1208008704 | bytes 4587520 | tf_op jit(solution)/shard_map/dot_general | solution.py:110
  173.7 1.1 copy.15
  174.8 0.7 copy.18
  175.5 0.1 copy_subtract_fusion
  175.6 0.7 copy.17
  (4 shorter events, 0.1 us)
Async XLA Ops:
  7.2 99.6 %reduce-scatter.2.cloned.1.call-start = ((), (), s32[]{:S(2)}) async-start(), calls=%async_computation.1 | async-start | bytes 1179648 | tf_op jit(solution)/shard_map/reduce_scatter | solution.py:108
  8.2 8.1 %collective-permute-start.1 = (f32[6,8,6,128]{3,1,2,0:T(8,128)S(1)}, f32[6,8,6,128]{3,1,2,0:T(8,128)S(1)}, u32[]{:S(2)}, u32[]{:S(2)}) collective-permute-start(f32[6,8,6,128]{3,1,2,0:T(8,128)S(1)} %get-tuple-element.12), channel_id=1, source_target_pairs={{0,8},{8,16},{16,24},{1,9},{9,17},{17,25},{2,10},{10,18},{18,26},{... | collective-permute-start | bytes 442376 | tf_op jit(solution)/shard_map/ppermute | solution.py:24
  13.2 7.2 %collective-permute-start = (f32[6,8,6,128]{3,1,2,0:T(8,128)S(1)}, f32[6,8,6,128]{3,1,2,0:T(8,128)S(1)}, u32[]{:S(2)}, u32[]{:S(2)}) collective-permute-start(f32[6,8,6,128]{3,1,2,0:T(8,128)S(1)} %get-tuple-element.11), channel_id=1, source_target_pairs={{8,0},{16,8},{24,16},{9,1},{17,9},{25,17},{10,2},{18,10},{26,18},{... | collective-permute-start | bytes 442376 | tf_op jit(solution)/shard_map/ppermute | solution.py:27
  20.5 4.6 %collective-permute-start.2 = (f32[20,6,6,128]{3,1,2,0:T(8,128)S(1)}, f32[20,6,6,128]{3,1,2,0:T(8,128)S(1)}, u32[]{:S(2)}, u32[]{:S(2)}) collective-permute-start(f32[20,6,6,128]{3,1,2,0:T(8,128)S(1)} %get-tuple-element.6), channel_id=1, source_target_pairs={{2,0},{4,2},{6,4},{3,1},{5,3},{7,5},{10,8},{12,10},{14,12},{11,9},... | collective-permute-start | bytes 1105928 | tf_op jit(solution)/shard_map/ppermute | solution.py:27
  21.8 9.7 %copy-start.3 = (f32[8,8,6]{1,0,2:T(8,128)S(1)}, f32[8,8,6]{1,0,2:T(8,128)}, u32[]{:S(2)}) copy-start(f32[8,8,6]{1,0,2:T(8,128)} %param.8) | copy-start | bytes 4612
  21.8 41.3 %copy-start.1 = (f32[8,8,6,128]{3,1,2,0:T(8,128)S(1)}, f32[8,8,6,128]{3,1,2,0:T(8,128)}, u32[]{:S(2)}) copy-start(f32[8,8,6,128]{3,1,2,0:T(8,128)} %param.5) | copy-start | bytes 589828
  21.8 41.3 %copy-start.2 = (f32[8,8,6,128]{3,1,2,0:T(8,128)S(1)}, f32[8,8,6,128]{3,1,2,0:T(8,128)}, u32[]{:S(2)}) copy-start(f32[8,8,6,128]{3,1,2,0:T(8,128)} %param.6) | copy-start | bytes 589828
  21.8 41.3 %copy-start.4 = (f32[128]{0:T(128)S(1)}, f32[128]{0:T(128)}, u32[]{:S(2)}) copy-start(f32[128]{0:T(128)} %param.9) | copy-start | bytes 1540
  21.8 4.6 %collective-permute-start.3 = (f32[20,6,6,128]{3,1,2,0:T(8,128)S(1)}, f32[20,6,6,128]{3,1,2,0:T(8,128)S(1)}, u32[]{:S(2)}, u32[]{:S(2)}) collective-permute-start(f32[20,6,6,128]{3,1,2,0:T(8,128)S(1)} %get-tuple-element.7), channel_id=1, source_target_pairs={{0,2},{2,4},{4,6},{1,3},{3,5},{5,7},{8,10},{10,12},{12,14},{9,11},... | collective-permute-start | bytes 1105928 | tf_op jit(solution)/shard_map/ppermute | solution.py:24
  26.7 31.7 %collective-permute-start.5 = (f32[20,20,6,128]{3,1,2,0:T(8,128)S(1)}, f32[20,20,6,128]{3,1,2,0:T(8,128)S(1)}, u32[]{:S(2)}, u32[]{:S(2)}) collective-permute-start(f32[20,20,6,128]{3,1,2,0:T(8,128)S(1)} %pad_maximum_fusion), channel_id=1, source_target_pairs={{0,1},{2,3},{4,5},{6,7},{8,9},{10,11},{12,13},{14,15},{16,17},{18,... | collective-permute-start | bytes 3686408 | tf_op jit(solution)/shard_map/ppermute | solution.py:24
  30.2 32.9 %collective-permute-start.4 = (f32[20,20,6,128]{3,1,2,0:T(8,128)S(1)}, f32[20,20,6,128]{3,1,2,0:T(8,128)S(1)}, u32[]{:S(2)}, u32[]{:S(2)}) collective-permute-start(f32[20,20,6,128]{3,1,2,0:T(8,128)S(1)} %pad_maximum_fusion), channel_id=1, source_target_pairs={{1,0},{3,2},{5,4},{7,6},{9,8},{11,10},{13,12},{15,14},{17,16},{19,... | collective-permute-start | bytes 3686408 | tf_op jit(solution)/shard_map/ppermute | solution.py:27
  63.1 1.9 %copy-start = (f32[8,8,6,2048]{3,1,2,0:T(8,128)S(1)}, f32[8,8,6,2048]{3,1,2,0:T(8,128)}, u32[]{:S(2)}) copy-start(f32[8,8,6,2048]{3,1,2,0:T(8,128)} %param.7) | copy-start | bytes 9437188
  68.1 75.7 %all-reduce.2.cloned.1.call-start = ((), (), s32[]{:S(2)}) async-start(), calls=%async_computation.2 | async-start | bytes 262144 | tf_op jit(solution)/shard_map/psum | solution.py:109
  106.8 62.1 %all-gather.2.cloned.1.call-start = ((), (), s32[]{:S(2)}) async-start(), calls=%async_computation.3 | async-start | bytes 1179648 | tf_op jit(solution)/shard_map/all_gather | solution.py:112
Sparse Core Ops, SparseCore 0:
  68.2 38.5 reduce-scatter.1
  109.1 34.6 all-reduce.1
  145.7 23.1 all-gather.1
where the time goes:
time: 183 us
  waiting for transfers between devices  128 us (70%)
  local copies, waits for them, and re-layouts  15.9 us (9%)
  starting transfers between devices  15.7 us (9%)
  between operations  13.9 us (8%)
  matrix products  7.81 us (4%)
    reduce_scatter x1, waiting for transfers between devices, shards(): lax.psum_scatter(partial_intersection, ('gy', 'gz'), scatter_dimension=0,...  38.7 us
    psum x1, waiting for transfers between devices, shards(): share = lax.psum(share, 'gx')  36.9 us
    ppermute x3, waiting for transfers between devices, with_halo(): lax.ppermute(lax.slice_in_dim(block, block.shape[dim] - width, None, axis...  30 us
    all_gather x1, waiting for transfers between devices, shards(): lax.all_gather(share, ('gy', 'gz'), axis=0, tiled=True)  14.8 us
    ppermute x3, starting transfers between devices, with_halo(): lax.ppermute(lax.slice_in_dim(block, block.shape[dim] - width, None, axis...  11.7 us
    ppermute x3, waiting for transfers between devices, with_halo(): lax.ppermute(lax.slice_in_dim(block, 0, width, axis=dim), axis, backward)  7.89 us
    unnamed x16, local copies, waits for them, and re-layouts  7.19 us
    dot_general x1, matrix products, shards(): jnp.dot(flat_occ, lax.all_gather(share, ('gy', 'gz'), axis=0, tiled=True)...  4.81 us
  transfers between devices with their start and end apart: 9, of which 8 were waited for; matrix products, arithmetic and copies ran while one was open for 6% of the time, Pallas kernels for 0%

commit v1 on v0

--- a/solution.py
+++ b/solution.py
@@ -14,6 +14,22 @@
 )
 damping = 0.1
 margin = 6
+
+
+def gather_around(x, axis, dim):
+    ways, here, step = (lax.axis_size(axis), lax.axis_index(axis), x.shape[dim])
+    shape = [n * ways if d == dim else n for d, n in enumerate(x.shape)]
+    full = lax.dynamic_update_slice_in_dim(jnp.zeros(shape, x.dtype), x, here * step, axis=dim)
+    going_up = going_down = x
+    for far in range(1, ways // 2 + 1):
+        going_up = lax.ppermute(going_up, axis, [(d, (d + 1) % ways) for d in range(ways)])
+        full = lax.dynamic_update_slice_in_dim(full, going_up, (here - far) % ways * step, axis=dim)
+        if 2 * far < ways:
+            going_down = lax.ppermute(going_down, axis, [(d, (d - 1) % ways) for d in range(ways)])
+            full = lax.dynamic_update_slice_in_dim(
+                full, going_down, (here + far) % ways * step, axis=dim
+            )
+    return full
 
 
 def with_halo(block, sides, width):
@@ -109,7 +125,7 @@
     share = lax.psum(share, "gx")
     removed = jnp.dot(
         flat_occ,
-        lax.all_gather(share, ("gy", "gz"), axis=0, tiled=True),
+        gather_around(share, ("gy", "gz"), 0),
         precision=lax.Precision.HIGHEST,
         preferred_element_type=jnp.float32,
     )

time: 183 us -> 190 us (1.038)
  starting transfers between devices: 15.7 us -> 24.6 us
  waiting for transfers between devices: 128 us -> 124 us
  local copies, waits for them, and re-layouts: 15.9 us -> 19 us
    all_gather x1 -> x0, waiting for transfers between devices: 14.8 us -> none  [shards(): lax.all_gather(share, ('gy', 'gz'), axis=0, tiled=True)]
    ppermute x0 -> x7, waiting for transfers between devices: none -> 10.1 us  [the longest x4 7.46 us: gather_around(): lax.ppermute(going_up, axis, [(d, (d + 1) % ways) for d in range(ways)])]
    ppermute x0 -> x7, starting transfers between devices: none -> 8.97 us  [the longest x4 8.28 us: gather_around(): lax.ppermute(going_up, axis, [(d, (d + 1) % ways) for d in range(ways)])]
    dynamic_update_slice x0 -> x8, local copies, waits for them, and re-layouts: none -> 2.86 us  [the longest x4 0.98 us: gather_around(): lax.dynamic_update_slice_in_dim(full, going_up, (here - far) % ways * ste...]
  transfers between devices with their start and end apart: 9 -> 15, of which waited for: 8 -> 11; matrix products, arithmetic and copies ran while one was open for 6% -> 8% of each run, Pallas kernels for 0% -> 0%
where the time goes in v1:
time: 190 us; the launch traced here: 189 us
  waiting for transfers between devices  124 us (65%)
  starting transfers between devices  24.6 us (13%)
  local copies, waits for them, and re-layouts  19 us (10%)
  between operations  14.3 us (8%)
  matrix products  6.62 us (3%)
    reduce_scatter x1, waiting for transfers between devices, shards(): lax.psum_scatter(partial_intersection, ('gy', 'gz'), scatter_dimension=0,...  38.7 us
    psum x1, waiting for transfers between devices, shards(): share = lax.psum(share, 'gx')  37 us
    ppermute x3, waiting for transfers between devices, with_halo(): lax.ppermute(lax.slice_in_dim(block, block.shape[dim] - width, None, axis...  30 us
    ppermute x3, starting transfers between devices, with_halo(): lax.ppermute(lax.slice_in_dim(block, block.shape[dim] - width, None, axis...  11.7 us
    ppermute x4, starting transfers between devices, gather_around(): lax.ppermute(going_up, axis, [(d, (d + 1) % ways) for d in range(ways)])  8.28 us
    ppermute x3, waiting for transfers between devices, with_halo(): lax.ppermute(lax.slice_in_dim(block, 0, width, axis=dim), axis, backward)  7.89 us
    ppermute x4, waiting for transfers between devices, gather_around(): lax.ppermute(going_up, axis, [(d, (d + 1) % ways) for d in range(ways)])  7.46 us
    unnamed x16, local copies, waits for them, and re-layouts  7.34 us
  transfers between devices with their start and end apart: 15, of which 11 were waited for; matrix products, arithmetic and copies ran while one was open for 8% of the time, Pallas kernels for 0%

profile of v1, /device:TPU:0, one launch (start us, length us, event | category | flops | bytes accessed | tf_op | source)
XLA Modules:
  0.0 189.5 jit_solution(12587301395120240177)
XLA Ops:
  7.2 0.0 reduce-scatter.2.cloned.1.call-start
  7.2 1.0 fusion.49
  8.2 5.0 %collective-permute-start.1 = (f32[6,8,6,128]{3,1,2,0:T(8,128)S(1)}, f32[6,8,6,128]{3,1,2,0:T(8,128)S(1)}, u32[]{:S(2)}, u32[]{:S(2)}) collective-permute-start(f32[6,8,6,128]{3,1,2,0:T(8,128)S(1)} %get-tuple-element.12), channel_id=1, source_target_pairs={{0,8},{8,16},{16,24},{1,9},{9,17},{17,25},{2,10},{10,18},{18,26},{... | collective-permute-start | bytes 442376 | tf_op jit(solution)/shard_map/ppermute | solution.py:40
  13.2 1.3 collective-permute-start
  14.5 1.8 collective-permute-done.1
  16.3 1.0 constant_dynamic-update-slice_fusion.1
  17.3 3.1 %collective-permute-done = f32[6,8,6,128]{3,1,2,0:T(8,128)S(1)} collective-permute-done((f32[6,8,6,128]{3,1,2,0:T(8,128)S(1)}, f32[6,8,6,128]{3,1,2,0:T(8,128)S(1)}, u32[]{:S(2)}, u32[]{:S(2)}) %collective-permute-start) | collective-permute-done | bytes 147488 | tf_op jit(solution)/shard_map/ppermute | solution.py:43
  20.4 0.1 fusion.48
  20.5 1.3 collective-permute-start.2
  21.8 0.0 copy-start.3
  21.8 0.0 copy-start.1
  21.8 0.0 copy-start.2
  21.8 0.0 copy-start.4
  21.8 3.2 %collective-permute-start.3 = (f32[20,6,6,128]{3,1,2,0:T(8,128)S(1)}, f32[20,6,6,128]{3,1,2,0:T(8,128)S(1)}, u32[]{:S(2)}, u32[]{:S(2)}) collective-permute-start(f32[20,6,6,128]{3,1,2,0:T(8,128)S(1)} %get-tuple-element.7), channel_id=1, source_target_pairs={{0,2},{2,4},{4,6},{1,3},{3,5},{5,7},{8,10},{10,12},{12,14},{9,11},... | collective-permute-start | bytes 1105928 | tf_op jit(solution)/shard_map/ppermute | solution.py:40
  25.0 0.0 collective-permute-done.2
  25.1 1.4 collective-permute-done.3
  26.5 0.2 pad_maximum_fusion
  26.7 3.5 %collective-permute-start.5 = (f32[20,20,6,128]{3,1,2,0:T(8,128)S(1)}, f32[20,20,6,128]{3,1,2,0:T(8,128)S(1)}, u32[]{:S(2)}, u32[]{:S(2)}) collective-permute-start(f32[20,20,6,128]{3,1,2,0:T(8,128)S(1)} %pad_maximum_fusion), channel_id=1, source_target_pairs={{0,1},{2,3},{4,5},{6,7},{8,9},{10,11},{12,13},{14,15},{16,17},{18,... | collective-permute-start | bytes 3686408 | tf_op jit(solution)/shard_map/ppermute | solution.py:40
  30.2 1.3 collective-permute-start.4
  31.5 0.0 copy-done.3
  31.6 26.8 %collective-permute-done.5 = f32[20,20,6,128]{3,1,2,0:T(8,128)S(1)} collective-permute-done((f32[20,20,6,128]{3,1,2,0:T(8,128)S(1)}, f32[20,20,6,128]{3,1,2,0:T(8,128)S(1)}, u32[]{:S(2)}, u32[]{:S(2)}) %collective-permute-start.5) | collective-permute-done | bytes 1228832 | tf_op jit(solution)/shard_map/ppermute | solution.py:40
  58.4 4.8 %collective-permute-done.4 = f32[20,20,6,128]{3,1,2,0:T(8,128)S(1)} collective-permute-done((f32[20,20,6,128]{3,1,2,0:T(8,128)S(1)}, f32[20,20,6,128]{3,1,2,0:T(8,128)S(1)}, u32[]{:S(2)}, u32[]{:S(2)}) %collective-permute-start.4) | collective-permute-done | bytes 1228832 | tf_op jit(solution)/shard_map/ppermute | solution.py:43
  63.1 0.0 copy-done.1
  63.1 0.0 copy-done.2
  63.1 0.0 copy-done.4
  63.1 0.0 copy-start
  63.2 0.9 fusion.10
  64.1 1.0 copy-done
  65.0 3.0 %convolution_bitcast_fusion = f32[2048,128]{0,1:T(8,128)} fusion(f32[8,8,6,128]{3,1,2,0:T(8,128)S(1)} %fusion.10, f32[8,8,6,2048]{3,1,2,0:T(8,128)S(1)} %copy-done), kind=kOutput, calls=%fused_computation | convolution fusion | flops 1207959552 | bytes 4390912 | tf_op jit(solution)/shard_map/dot_general | solution.py:117
  68.1 0.0 reduce-scatter.2.cloned.1.call-update
  68.1 0.0 all-reduce.2.cloned.1.call-start
  68.1 38.7 %reduce-scatter.2.cloned.1.call-done = f32[256,128]{0,1:T(8,128)} async-done(((f32[2048,128]{0,1:T(8,128)}), f32[256,128]{0,1:T(8,128)}) %reduce-scatter.2.cloned.1.call-update) | async-done | bytes 131088 | tf_op jit(solution)/shard_map/reduce_scatter | solution.py:124
  106.8 0.0 all-reduce.2.cloned.1.call-update
  106.8 37.0 %all-reduce.2.cloned.1.call-done = f32[256,128]{0,1:T(8,128)} async-done(((f32[256,128]{0,1:T(8,128)}), f32[256,128]{0,1:T(8,128)}) %all-reduce.2.cloned.1.call-update) | async-done | bytes 131088 | tf_op jit(solution)/shard_map/psum | solution.py:125
  143.8 0.0 collective-permute-start.7
  143.8 2.0 %collective-permute-start.6 = (f32[256,128]{0,1:T(8,128)}, f32[256,128]{0,1:T(8,128)}, u32[]{:S(2)}, u32[]{:S(2)}) collective-permute-start(f32[256,128]{0,1:T(8,128)} %all-reduce.2.cloned.1.call-done), channel_id=1, source_target_pairs={{0,1},{1,2},{2,3},{3,4},{4,5},{5,6},{6,7},{7,0},{8,9},{9,10},{10,1... | collective-permute-start | bytes 393224 | tf_op jit(solution)/shard_map/ppermute | solution.py:25
  145.8 3.9 %copy.13 = f32[8,8,6,2048]{3,2,1,0:T(8,128)} copy(f32[8,8,6,2048]{3,1,2,0:T(8,128)S(1)} %copy-done) | data formatting | bytes 6291456 | tf_op args[2]
  149.8 3.1 %reshape.16 = f32[384,2048]{1,0:T(8,128)S(1)} reshape(f32[8,8,6,2048]{3,2,1,0:T(8,128)} %copy.13) | data formatting | bytes 6291456 | tf_op jit(solution)/shard_map/reshape | solution.py:112
  152.9 0.7 copy.12
  153.6 1.6 reshape.15
  155.3 1.1 copy.14
  156.3 0.1 broadcast_in_dim.2
  156.4 0.9 constant_dynamic-update-slice_fusion.14
  157.4 0.0 collective-permute-done.7
  157.4 0.7 collective-permute-start.9
  158.0 0.0 collective-permute-done.6
  158.1 1.4 collective-permute-start.8
  159.5 0.9 constant_dynamic-update-slice_fusion.13
  160.4 0.9 constant_dynamic-update-slice_fusion.12
  161.3 2.7 %collective-permute-done.9 = f32[256,128]{0,1:T(8,128)S(1)} collective-permute-done((f32[256,128]{0,1:T(8,128)}, f32[256,128]{0,1:T(8,128)S(1)}, u32[]{:S(2)}, u32[]{:S(2)}) %collective-permute-start.9) | collective-permute-done | bytes 131104 | tf_op jit(solution)/shard_map/ppermute | solution.py:28
  164.0 0.0 collective-permute-start.11
  164.0 0.6 collective-permute-done.8
  164.6 2.4 %collective-permute-start.10 = (f32[256,128]{0,1:T(8,128)S(1)}, f32[256,128]{0,1:T(8,128)S(1)}, u32[]{:S(2)}, u32[]{:S(2)}) collective-permute-start(f32[256,128]{0,1:T(8,128)S(1)} %collective-permute-done.8), channel_id=1, source_target_pairs={{0,1},{1,2},{2,3},{3,4},{4,5},{5,6},{6,7},{7,0},{8,9},{9,10},{10,1... | collective-permute-start | bytes 393224 | tf_op jit(solution)/shard_map/ppermute | solution.py:25
  167.1 3.8 %collective-permute-done.10 = f32[256,128]{0,1:T(8,128)S(1)} collective-permute-done((f32[256,128]{0,1:T(8,128)S(1)}, f32[256,128]{0,1:T(8,128)S(1)}, u32[]{:S(2)}, u32[]{:S(2)}) %collective-permute-start.10) | collective-permute-done | bytes 131104 | tf_op jit(solution)/shard_map/ppermute | solution.py:25
  170.9 2.5 %collective-permute-start.12 = (f32[256,128]{0,1:T(8,128)S(1)}, f32[256,128]{0,1:T(8,128)S(1)}, u32[]{:S(2)}, u32[]{:S(2)}) collective-permute-start(f32[256,128]{0,1:T(8,128)S(1)} %collective-permute-done.10), channel_id=1, source_target_pairs={{0,1},{1,2},{2,3},{3,4},{4,5},{5,6},{6,7},{7,0},{8,9},{9,10},{10,1... | collective-permute-start | bytes 393224 | tf_op jit(solution)/shard_map/ppermute | solution.py:25
  173.4 0.0 collective-permute-done.11
  173.4 3.0 %collective-permute-done.12 = f32[256,128]{0,1:T(8,128)S(1)} collective-permute-done((f32[256,128]{0,1:T(8,128)S(1)}, f32[256,128]{0,1:T(8,128)S(1)}, u32[]{:S(2)}, u32[]{:S(2)}) %collective-permute-start.12) | collective-permute-done | bytes 131104 | tf_op jit(solution)/shard_map/ppermute | solution.py:25
  176.4 3.6 %fusion = f32[384,128]{0,1:T(8,128)} fusion(f32[384,128]{0,1:T(8,128)S(1)} %copy.14, f32[2048,128]{0,1:T(8,128)S(1)} %constant_dynamic-update-slice_fusion.7, f32[384,2048]{1,0:T(8,128)S(1)} %reshape.16), kind=kOutput, calls=%fused_computation.23 | convolution fusion | flops 1208008704 | bytes 4587520 | tf_op jit(solution)/shard_map/dot_general | solution.py:126
  180.0 1.1 copy.15
  181.1 0.7 copy.18
  181.8 0.1 copy_subtract_fusion
  181.9 0.7 copy.17
  (9 shorter events, 0.1 us)
Async XLA Ops:
  7.2 99.6 %reduce-scatter.2.cloned.1.call-start = ((), (), s32[]{:S(2)}) async-start(), calls=%async_computation.1 | async-start | bytes 1179648 | tf_op jit(solution)/shard_map/reduce_scatter | solution.py:124
  8.2 8.1 %collective-permute-start.1 = (f32[6,8,6,128]{3,1,2,0:T(8,128)S(1)}, f32[6,8,6,128]{3,1,2,0:T(8,128)S(1)}, u32[]{:S(2)}, u32[]{:S(2)}) collective-permute-start(f32[6,8,6,128]{3,1,2,0:T(8,128)S(1)} %get-tuple-element.12), channel_id=1, source_target_pairs={{0,8},{8,16},{16,24},{1,9},{9,17},{17,25},{2,10},{10,18},{18,26},{... | collective-permute-start | bytes 442376 | tf_op jit(solution)/shard_map/ppermute | solution.py:40
  13.2 7.2 %collective-permute-start = (f32[6,8,6,128]{3,1,2,0:T(8,128)S(1)}, f32[6,8,6,128]{3,1,2,0:T(8,128)S(1)}, u32[]{:S(2)}, u32[]{:S(2)}) collective-permute-start(f32[6,8,6,128]{3,1,2,0:T(8,128)S(1)} %get-tuple-element.11), channel_id=1, source_target_pairs={{8,0},{16,8},{24,16},{9,1},{17,9},{25,17},{10,2},{18,10},{26,18},{... | collective-permute-start | bytes 442376 | tf_op jit(solution)/shard_map/ppermute | solution.py:43
  20.5 4.6 %collective-permute-start.2 = (f32[20,6,6,128]{3,1,2,0:T(8,128)S(1)}, f32[20,6,6,128]{3,1,2,0:T(8,128)S(1)}, u32[]{:S(2)}, u32[]{:S(2)}) collective-permute-start(f32[20,6,6,128]{3,1,2,0:T(8,128)S(1)} %get-tuple-element.6), channel_id=1, source_target_pairs={{2,0},{4,2},{6,4},{3,1},{5,3},{7,5},{10,8},{12,10},{14,12},{11,9},... | collective-permute-start | bytes 1105928 | tf_op jit(solution)/shard_map/ppermute | solution.py:43
  21.8 9.7 %copy-start.3 = (f32[8,8,6]{1,0,2:T(8,128)S(1)}, f32[8,8,6]{1,0,2:T(8,128)}, u32[]{:S(2)}) copy-start(f32[8,8,6]{1,0,2:T(8,128)} %param.8) | copy-start | bytes 4612
  21.8 41.3 %copy-start.1 = (f32[8,8,6,128]{3,1,2,0:T(8,128)S(1)}, f32[8,8,6,128]{3,1,2,0:T(8,128)}, u32[]{:S(2)}) copy-start(f32[8,8,6,128]{3,1,2,0:T(8,128)} %param.5) | copy-start | bytes 589828
  21.8 41.3 %copy-start.2 = (f32[8,8,6,128]{3,1,2,0:T(8,128)S(1)}, f32[8,8,6,128]{3,1,2,0:T(8,128)}, u32[]{:S(2)}) copy-start(f32[8,8,6,128]{3,1,2,0:T(8,128)} %param.6) | copy-start | bytes 589828
  21.8 41.3 %copy-start.4 = (f32[128]{0:T(128)S(1)}, f32[128]{0:T(128)}, u32[]{:S(2)}) copy-start(f32[128]{0:T(128)} %param.9) | copy-start | bytes 1540
  21.8 4.6 %collective-permute-start.3 = (f32[20,6,6,128]{3,1,2,0:T(8,128)S(1)}, f32[20,6,6,128]{3,1,2,0:T(8,128)S(1)}, u32[]{:S(2)}, u32[]{:S(2)}) collective-permute-start(f32[20,6,6,128]{3,1,2,0:T(8,128)S(1)} %get-tuple-element.7), channel_id=1, source_target_pairs={{0,2},{2,4},{4,6},{1,3},{3,5},{5,7},{8,10},{10,12},{12,14},{9,11},... | collective-permute-start | bytes 1105928 | tf_op jit(solution)/shard_map/ppermute | solution.py:40
  26.7 31.7 %collective-permute-start.5 = (f32[20,20,6,128]{3,1,2,0:T(8,128)S(1)}, f32[20,20,6,128]{3,1,2,0:T(8,128)S(1)}, u32[]{:S(2)}, u32[]{:S(2)}) collective-permute-start(f32[20,20,6,128]{3,1,2,0:T(8,128)S(1)} %pad_maximum_fusion), channel_id=1, source_target_pairs={{0,1},{2,3},{4,5},{6,7},{8,9},{10,11},{12,13},{14,15},{16,17},{18,... | collective-permute-start | bytes 3686408 | tf_op jit(solution)/shard_map/ppermute | solution.py:40
  30.2 32.9 %collective-permute-start.4 = (f32[20,20,6,128]{3,1,2,0:T(8,128)S(1)}, f32[20,20,6,128]{3,1,2,0:T(8,128)S(1)}, u32[]{:S(2)}, u32[]{:S(2)}) collective-permute-start(f32[20,20,6,128]{3,1,2,0:T(8,128)S(1)} %pad_maximum_fusion), channel_id=1, source_target_pairs={{1,0},{3,2},{5,4},{7,6},{9,8},{11,10},{13,12},{15,14},{17,16},{19,... | collective-permute-start | bytes 3686408 | tf_op jit(solution)/shard_map/ppermute | solution.py:43
  63.1 1.9 copy-start
  68.1 75.7 %all-reduce.2.cloned.1.call-start = ((), (), s32[]{:S(2)}) async-start(), calls=%async_computation.2 | async-start | bytes 262144 | tf_op jit(solution)/shard_map/psum | solution.py:125
  143.8 13.6 %collective-permute-start.7 = (f32[256,128]{0,1:T(8,128)}, f32[256,128]{0,1:T(8,128)}, u32[]{:S(2)}, u32[]{:S(2)}) collective-permute-start(f32[256,128]{0,1:T(8,128)} %all-reduce.2.cloned.1.call-done), channel_id=1, source_target_pairs={{0,7},{1,0},{2,1},{3,2},{4,3},{5,4},{6,5},{7,6},{8,15},{9,8},{10,9... | collective-permute-start | bytes 393224 | tf_op jit(solution)/shard_map/ppermute | solution.py:28
  143.8 14.2 %collective-permute-start.6 = (f32[256,128]{0,1:T(8,128)}, f32[256,128]{0,1:T(8,128)}, u32[]{:S(2)}, u32[]{:S(2)}) collective-permute-start(f32[256,128]{0,1:T(8,128)} %all-reduce.2.cloned.1.call-done), channel_id=1, source_target_pairs={{0,1},{1,2},{2,3},{3,4},{4,5},{5,6},{6,7},{7,0},{8,9},{9,10},{10,1... | collective-permute-start | bytes 393224 | tf_op jit(solution)/shard_map/ppermute | solution.py:25
  157.4 6.6 %collective-permute-start.9 = (f32[256,128]{0,1:T(8,128)}, f32[256,128]{0,1:T(8,128)S(1)}, u32[]{:S(2)}, u32[]{:S(2)}) collective-permute-start(f32[256,128]{0,1:T(8,128)} %collective-permute-done.7), channel_id=1, source_target_pairs={{0,7},{1,0},{2,1},{3,2},{4,3},{5,4},{6,5},{7,6},{8,15},{9,8},{10,9... | collective-permute-start | bytes 393224 | tf_op jit(solution)/shard_map/ppermute | solution.py:28
  158.1 6.6 %collective-permute-start.8 = (f32[256,128]{0,1:T(8,128)}, f32[256,128]{0,1:T(8,128)S(1)}, u32[]{:S(2)}, u32[]{:S(2)}) collective-permute-start(f32[256,128]{0,1:T(8,128)} %collective-permute-done.6), channel_id=1, source_target_pairs={{0,1},{1,2},{2,3},{3,4},{4,5},{5,6},{6,7},{7,0},{8,9},{9,10},{10,1... | collective-permute-start | bytes 393224 | tf_op jit(solution)/shard_map/ppermute | solution.py:25
  164.0 9.4 %collective-permute-start.11 = (f32[256,128]{0,1:T(8,128)S(1)}, f32[256,128]{0,1:T(8,128)S(1)}, u32[]{:S(2)}, u32[]{:S(2)}) collective-permute-start(f32[256,128]{0,1:T(8,128)S(1)} %collective-permute-done.9), channel_id=1, source_target_pairs={{0,7},{1,0},{2,1},{3,2},{4,3},{5,4},{6,5},{7,6},{8,15},{9,8},{10,9... | collective-permute-start | bytes 393224 | tf_op jit(solution)/shard_map/ppermute | solution.py:28
  164.6 6.3 %collective-permute-start.10 = (f32[256,128]{0,1:T(8,128)S(1)}, f32[256,128]{0,1:T(8,128)S(1)}, u32[]{:S(2)}, u32[]{:S(2)}) collective-permute-start(f32[256,128]{0,1:T(8,128)S(1)} %collective-permute-done.8), channel_id=1, source_target_pairs={{0,1},{1,2},{2,3},{3,4},{4,5},{5,6},{6,7},{7,0},{8,9},{9,10},{10,1... | collective-permute-start | bytes 393224 | tf_op jit(solution)/shard_map/ppermute | solution.py:25
  170.9 5.5 %collective-permute-start.12 = (f32[256,128]{0,1:T(8,128)S(1)}, f32[256,128]{0,1:T(8,128)S(1)}, u32[]{:S(2)}, u32[]{:S(2)}) collective-permute-start(f32[256,128]{0,1:T(8,128)S(1)} %collective-permute-done.10), channel_id=1, source_target_pairs={{0,1},{1,2},{2,3},{3,4},{4,5},{5,6},{6,7},{7,0},{8,9},{9,10},{10,1... | collective-permute-start | bytes 393224 | tf_op jit(solution)/shard_map/ppermute | solution.py:25
Sparse Core Ops, SparseCore 0:
  68.2 38.5 reduce-scatter.1
  109.1 34.6 all-reduce.1
